TPU v7x, 32 devices: a whole 2x2x4 slice. The times are simulated.
32 devices in a mesh: ctx: 8 (over y, x, core), ch: 4 (over z).
Axes of the slice: x: 2, y: 2, z: 4, core: 2. Of those that a mesh axis runs over, the one named last changes fastest.
Arguments:
- query_act: bfloat16 [2048, 8192], P('ctx', 'ch'), may hold values from -6 to 6
- key_act: bfloat16 [2048, 8192], P('ctx', 'ch'), may hold values from -6 to 6
- value_act: bfloat16 [2048, 8192], P('ctx', 'ch'), may hold values from -6 to 6
- out_grad: bfloat16 [2048, 8192], P('ctx', 'ch'), may hold values from -6 to 6
- out_weight: bfloat16 [8192, 8192], P('ctx', 'ch'), may hold values from -0.0625 to 0.0625
- token_mask: int32 [2048], P('ctx'), may hold values from 0 to 1, as said below
- decay_rate: float32 [16, 8192], P(None, 'ch'), may hold values from 4.8828125e-05 to 0.033
- residue: float32 [16, 8192], P(None, 'ch'), may hold values from -75 to 75
Outputs:
- query_grad: bfloat16 [2048, 8192], P('ctx', 'ch')
- key_grad: bfloat16 [2048, 8192], P('ctx', 'ch')
- value_grad: bfloat16 [2048, 8192], P('ctx', 'ch')
- filter_grad: float32 [16, 8192], P(None, 'ch')
Inputs may be any that keep to these rules, and one draw needn't show every extreme that they name: `token_mask`: 1 marks a valid token; within each aligned run of 64 positions the valid tokens come first.
All inputs are finite; a program needn't handle non-finite values.
Results may differ from a plain program's by a relative error of at most 0.0015.
Values may be sent and summed in bfloat16 or wider, within the bound.
A program may use at most 192 MiB of HBM per device.

v0:
```python
import jax
import jax.numpy as jnp
from jax import lax
from jax.sharding import PartitionSpec as P


def carried_in(shard, axis, combine, identity, reverse):
    devices, here = (lax.axis_size(axis), lax.axis_index(axis))
    everything = jax.tree.map(lambda part: lax.all_gather(part, axis), shard)
    start = jax.tree.map(
        lambda part, zero: jnp.broadcast_to(jnp.asarray(zero, part.dtype), part.shape),
        shard,
        identity,
    )

    def turn(k, before):
        at = devices - 1 - k if reverse else k
        reached = at > here if reverse else at < here
        new = combine(before, jax.tree.map(lambda part: part[at], everything))
        return jax.tree.map(lambda a, b: jnp.where(reached, a, b), new, before)

    return lax.fori_loop(0, devices, turn, start)


def chain_join(earlier, later):
    return (earlier[0] * later[0], later[0] * earlier[1] + later[1])


def body(query_act, key_act, value_act, out_grad, out_weight, token_mask, decay_rate, residue):
    rows_block = 64
    tokens_here = query_act.shape[0]
    chans = query_act.shape[1]
    modes = decay_rate.shape[0]
    blocks = tokens_here // rows_block
    live = token_mask.astype(jnp.float32)[:, None]
    inputs = live * key_act.astype(jnp.float32) * value_act.astype(jnp.float32)
    root_gain = jnp.sqrt(-jnp.expm1(-2.0 * decay_rate))
    filter_gain = residue * root_gain
    places = jnp.arange(rows_block).astype(jnp.float32)[:, None, None]
    rising = jnp.exp(decay_rate[None] * places)
    falling = jnp.exp(-decay_rate[None] * places)
    step_decay = jnp.exp(-decay_rate)
    trailing = jnp.exp(-decay_rate[None] * (rows_block - places))
    row_ids = lax.broadcasted_iota(jnp.int32, (rows_block, rows_block), 0)
    col_ids = lax.broadcasted_iota(jnp.int32, (rows_block, rows_block), 1)
    lower_ones = (row_ids >= col_ids).astype(jnp.float32)
    upper_ones = (row_ids <= col_ids).astype(jnp.float32)
    zeros = jnp.zeros((modes, chans), jnp.float32)

    def forward_block(carried, block_in):
        scaled = (rising * block_in[:, None, :]).reshape(rows_block, modes * chans)
        summed = jnp.dot(lower_ones, scaled, precision=lax.Precision.HIGHEST).reshape(
            rows_block, modes, chans
        )
        states = falling * summed + falling * step_decay[None] * carried[None]
        return (states[-1], jnp.sum(filter_gain[None] * states, axis=1))

    end_state, conv_local = lax.scan(
        forward_block, zeros, inputs.reshape(blocks, rows_block, chans)
    )
    conv_local = conv_local.reshape(tokens_here, chans)
    full_grad = lax.all_gather(out_grad, "ch", axis=1, tiled=True)
    gate_grad = jnp.dot(
        full_grad,
        lax.all_gather(out_weight, "ctx", axis=0, tiled=True),
        preferred_element_type=jnp.float32,
    )
    conv_grad = gate_grad * query_act.astype(jnp.float32)

    def backward_block(carry, block_in):
        carried, running = carry
        grad_blk, input_blk = block_in
        scaled = (falling * grad_blk[:, None, :]).reshape(rows_block, modes * chans)
        summed = jnp.dot(upper_ones, scaled, precision=lax.Precision.HIGHEST).reshape(
            rows_block, modes, chans
        )
        states = rising * summed + trailing * carried[None]
        running = running + jnp.sum(input_blk[:, None, :] * states, axis=0)
        return ((states[0], running), jnp.sum(filter_gain[None] * states, axis=1))

    (start_state, filter_local), grad_local = lax.scan(
        backward_block,
        (zeros, zeros),
        (conv_grad.reshape(blocks, rows_block, chans), inputs.reshape(blocks, rows_block, chans)),
        reverse=True,
    )
    grad_local = grad_local.reshape(tokens_here, chans)
    span_decay = jnp.exp(-decay_rate * tokens_here)
    forward_in = carried_in(
        (span_decay, end_state), "ctx", chain_join, (jnp.ones_like(span_decay), zeros), False
    )[1]
    backward_in = carried_in(
        (span_decay, start_state), "ctx", chain_join, (jnp.ones_like(span_decay), zeros), True
    )[1]
    token_places = jnp.arange(tokens_here).astype(jnp.float32)[:, None, None]
    conv = conv_local + jnp.sum(
        jnp.exp(-decay_rate[None] * (token_places + 1.0)) * (filter_gain * forward_in)[None], axis=1
    )
    input_grad = grad_local + jnp.sum(
        jnp.exp(-decay_rate[None] * (tokens_here - token_places))
        * (filter_gain * backward_in)[None],
        axis=1,
    )
    query_grad = (gate_grad * conv).astype(jnp.bfloat16)
    key_grad = (live * input_grad * value_act.astype(jnp.float32)).astype(jnp.bfloat16)
    value_grad = (live * input_grad * key_act.astype(jnp.float32)).astype(jnp.bfloat16)
    filter_terms = root_gain * (filter_local + backward_in * step_decay * end_state)
    filter_grad = lax.psum(filter_terms, "ctx")
    return (query_grad, key_grad, value_grad, filter_grad)


def solution(mesh):
    placed = (
        P("ctx", "ch"),
        P("ctx", "ch"),
        P("ctx", "ch"),
        P("ctx", "ch"),
        P("ctx", "ch"),
        P("ctx"),
        P(None, "ch"),
        P(None, "ch"),
    )
    return jax.shard_map(
        body,
        mesh=mesh,
        in_specs=placed,
        out_specs=(P("ctx", "ch"), P("ctx", "ch"), P("ctx", "ch"), P(None, "ch")),
        check_vma=False,
    )
```

profile of v0, /device:TPU:0, one launch (start us, length us, event | category | flops | bytes accessed | tf_op | source)
XLA Modules:
  0.0 719.4 jit_solution(11028100770254350850)
XLA Ops:
  14.7 100.9 %while.67 = (s32[]{:T(128)}, f32[16,2048]{1,0:T(8,128)S(1)}, f32[4,64,2048]{2,1,0:T(8,128)}, f32[4,64,2048]{2,1,0:T(8,128)S(1)}, f32[16,2048]{1,0:T(8,128)S(1)},...) while((s32[]{:T(128)}, f32[16,2048]{1,0:T(8,128)S(1)}, ...), condition=%wide.region_2.3_spmd.clone.clone, body=%wide.region_0.2_spmd.clone.clone.sunk | while | flops 1629364224 | bytes 79561336 | solution.py:58
  16.1 5.0 copy.28
  21.2 8.5 %fusion.52 = f32[32768,64]{0,1:T(8,128)S(1)} fusion(f32[64,32768]{1,0:T(8,128)S(1)} %bitcast.141), kind=kOutput, calls=%fused_computation.23.clone.1 | convolution fusion | flops 1610620928 | bytes 16777216 | tf_op jit(solution)/shard_map/while/body/eval_jaxpr/dot_general | solution.py:52
  29.7 5.0 copy.29
  41.3 5.0 copy.28
  46.3 8.5 %fusion.52 = f32[32768,64]{0,1:T(8,128)S(1)} fusion(f32[64,32768]{1,0:T(8,128)S(1)} %bitcast.141), kind=kOutput, calls=%fused_computation.23.clone.1 | convolution fusion | flops 1610620928 | bytes 16777216 | tf_op jit(solution)/shard_map/while/body/eval_jaxpr/dot_general | solution.py:52
  54.8 5.0 copy.29
  66.4 5.0 copy.28
  71.5 8.5 %fusion.52 = f32[32768,64]{0,1:T(8,128)S(1)} fusion(f32[64,32768]{1,0:T(8,128)S(1)} %bitcast.141), kind=kOutput, calls=%fused_computation.23.clone.1 | convolution fusion | flops 1610620928 | bytes 16777216 | tf_op jit(solution)/shard_map/while/body/eval_jaxpr/dot_general | solution.py:52
  80.0 5.0 copy.29
  91.6 5.0 copy.28
  96.6 8.5 %fusion.52 = f32[32768,64]{0,1:T(8,128)S(1)} fusion(f32[64,32768]{1,0:T(8,128)S(1)} %bitcast.141), kind=kOutput, calls=%fused_computation.23.clone.1 | convolution fusion | flops 1610620928 | bytes 16777216 | tf_op jit(solution)/shard_map/while/body/eval_jaxpr/dot_general | solution.py:52
  117.6 136.5 %all-gather.11.cloned.1.call-done = bf16[8192,2048]{1,0:T(8,128)(2,1)} async-done(((bf16[1024,2048]{1,0:T(8,128)(2,1)}), bf16[8192,2048]{1,0:T(8,128)(2,1)}) %all-gather.11.cloned.1.call-update) | async-done | bytes 33554448 | tf_op jit(solution)/shard_map/all_gather | solution.py:65
  254.1 17.9 %convert_multiply_fusion.4 = (f32[256,2048]{1,0:T(8,128)}, f32[256,2048]{1,0:T(8,128)}) fusion(bf16[256,2048]{1,0:T(8,128)(2,1)} %param.16, bf16[256,8192]{1,0:T(8,128)(2,1)} %all-gather.9.cloned.1.call-done, bf16[8192,2048]{1,0:T(8,128)(2,1)} %all-gather.11.cloned.1.call-done), kind=kOutput, calls=%fused_computation.57 | convolution fusion | flops 8590983168 | bytes 42991616 | tf_op jit(solution)/shard_map/dot_general | solution.py:63
  274.3 343.8 %while.68 = (s32[]{:T(128)}, f32[16,2048]{1,0:T(8,128)}, f32[16,2048]{1,0:T(8,128)}, f32[4,64,2048]{2,1,0:T(8,128)}, f32[4,64,2048]{2,1,0:T(8,128)}, /*index=5*/...) while((s32[]{:T(128)}, f32[16,2048]{1,0:T(8,128)}, ...), condition=%wide.region_9.10_spmd.clone.clone.clone, body=%wide.region_6.0_spmd.clone.clone.clone.sunk | while | flops 1639882752 | bytes 212862208 | solution.py:81
  283.5 8.8 %fusion.55 = f32[32768,64]{0,1:T(8,128)S(1)} fusion(f32[64,32768]{1,0:T(8,128)S(1)} %bitcast.143), kind=kOutput, calls=%fused_computation.41.clone.1 | convolution fusion | flops 1610620928 | bytes 16777216 | tf_op jit(solution)/shard_map/while/body/eval_jaxpr/dot_general | solution.py:74
  292.3 8.0 %copy.31 = f32[8,8,16,2048]{3,2,1,0:T(8,128)} copy(f32[8,8,16,2048]{3,1,2,0:T(8,128)S(1)} %bitcast.140) | data formatting | bytes 16777216 | tf_op jit(solution)/shard_map/while
  300.3 10.9 %multiply_reduce_fusion.7 = (f32[64,2048]{1,0:T(8,128)S(1)}, f32[64,16,2048]{2,1,0:T(8,128)}, f32[64,16,2048]{2,1,0:T(8,128)S(1)}, f32[64,16,2048]{2,1,0:T(8,128)}) fusion(f32[16,2048]{1,0:T(8,128)} %copy-done.7, f32[16,2048]{1,0:T(8,128)} %get-tuple-element.1005, f32[64]{0:T(128)S(1)} %get-tuple-element.1028, f32[16,2048]{1,0:T(8,128)} %copy-done, ...), kind=kLoop, calls=%fused_computation.35.clone.1 | loop fusion | flops 14548992 | bytes 34603520 | tf_op jit(solution)/shard_map/while/body/eval_jaxpr/reduce_sum | solution.py:79
  317.1 11.7 %copy.32 = f32[8,8,16,2048]{3,1,2,0:T(8,128)} copy(f32[8,8,16,2048]{3,2,1,0:T(8,128)} %bitcast.148) | data formatting | bytes 16777216 | tf_op jit(solution)/shard_map/while
  328.7 11.7 %copy.33 = f32[8,8,16,2048]{3,1,2,0:T(8,128)} copy(f32[8,8,16,2048]{3,2,1,0:T(8,128)} %bitcast.145) | data formatting | bytes 16777216 | tf_op jit(solution)/shard_map/while
  340.4 8.2 %copy.34 = f32[8,8,16,2048]{3,1,2,0:T(8,128)} copy(f32[8,8,16,2048]{3,2,1,0:T(8,128)S(1)} %bitcast.144) | data formatting | bytes 16777216 | tf_op jit(solution)/shard_map/while
  348.6 9.5 %fusion.56 = f32[32768]{0:T(1024)S(1)} fusion(f32[64,32768]{1,0:T(8,128)} %bitcast.149, f32[64,32768]{1,0:T(8,128)} %bitcast.150, f32[32768,64]{0,1:T(8,128)S(1)} %fusion.55, f32[64,32768]{1,0:T(8,128)} %bitcast.151, f32[32768]{0:T(1024)S(1)} %bitcast.153), kind=kLoop, calls=%fused_computation.31.clone.1 | loop fusion | flops 10452992 | bytes 33816576 | tf_op jit(solution)/shard_map/while/body/eval_jaxpr/reduce_sum | solution.py:78
  368.4 9.0 %fusion.55 = f32[32768,64]{0,1:T(8,128)S(1)} fusion(f32[64,32768]{1,0:T(8,128)S(1)} %bitcast.143), kind=kOutput, calls=%fused_computation.41.clone.1 | convolution fusion | flops 1610620928 | bytes 16777216 | tf_op jit(solution)/shard_map/while/body/eval_jaxpr/dot_general | solution.py:74
  377.4 8.0 %copy.31 = f32[8,8,16,2048]{3,2,1,0:T(8,128)} copy(f32[8,8,16,2048]{3,1,2,0:T(8,128)S(1)} %bitcast.140) | data formatting | bytes 16777216 | tf_op jit(solution)/shard_map/while
  385.4 10.7 %multiply_reduce_fusion.7 = (f32[64,2048]{1,0:T(8,128)S(1)}, f32[64,16,2048]{2,1,0:T(8,128)}, f32[64,16,2048]{2,1,0:T(8,128)S(1)}, f32[64,16,2048]{2,1,0:T(8,128)}) fusion(f32[16,2048]{1,0:T(8,128)} %copy-done.7, f32[16,2048]{1,0:T(8,128)} %get-tuple-element.1005, f32[64]{0:T(128)S(1)} %get-tuple-element.1028, f32[16,2048]{1,0:T(8,128)} %copy-done, ...), kind=kLoop, calls=%fused_computation.35.clone.1 | loop fusion | flops 14548992 | bytes 34603520 | tf_op jit(solution)/shard_map/while/body/eval_jaxpr/reduce_sum | solution.py:79
  402.0 11.7 %copy.32 = f32[8,8,16,2048]{3,1,2,0:T(8,128)} copy(f32[8,8,16,2048]{3,2,1,0:T(8,128)} %bitcast.148) | data formatting | bytes 16777216 | tf_op jit(solution)/shard_map/while
  413.6 11.7 %copy.33 = f32[8,8,16,2048]{3,1,2,0:T(8,128)} copy(f32[8,8,16,2048]{3,2,1,0:T(8,128)} %bitcast.145) | data formatting | bytes 16777216 | tf_op jit(solution)/shard_map/while
  425.3 8.2 %copy.34 = f32[8,8,16,2048]{3,1,2,0:T(8,128)} copy(f32[8,8,16,2048]{3,2,1,0:T(8,128)S(1)} %bitcast.144) | data formatting | bytes 16777216 | tf_op jit(solution)/shard_map/while
  433.6 9.5 %fusion.56 = f32[32768]{0:T(1024)S(1)} fusion(f32[64,32768]{1,0:T(8,128)} %bitcast.149, f32[64,32768]{1,0:T(8,128)} %bitcast.150, f32[32768,64]{0,1:T(8,128)S(1)} %fusion.55, f32[64,32768]{1,0:T(8,128)} %bitcast.151, f32[32768]{0:T(1024)S(1)} %bitcast.153), kind=kLoop, calls=%fused_computation.31.clone.1 | loop fusion | flops 10452992 | bytes 33816576 | tf_op jit(solution)/shard_map/while/body/eval_jaxpr/reduce_sum | solution.py:78
  453.5 8.8 %fusion.55 = f32[32768,64]{0,1:T(8,128)S(1)} fusion(f32[64,32768]{1,0:T(8,128)S(1)} %bitcast.143), kind=kOutput, calls=%fused_computation.41.clone.1 | convolution fusion | flops 1610620928 | bytes 16777216 | tf_op jit(solution)/shard_map/while/body/eval_jaxpr/dot_general | solution.py:74
  462.2 8.0 %copy.31 = f32[8,8,16,2048]{3,2,1,0:T(8,128)} copy(f32[8,8,16,2048]{3,1,2,0:T(8,128)S(1)} %bitcast.140) | data formatting | bytes 16777216 | tf_op jit(solution)/shard_map/while
  470.2 10.7 %multiply_reduce_fusion.7 = (f32[64,2048]{1,0:T(8,128)S(1)}, f32[64,16,2048]{2,1,0:T(8,128)}, f32[64,16,2048]{2,1,0:T(8,128)S(1)}, f32[64,16,2048]{2,1,0:T(8,128)}) fusion(f32[16,2048]{1,0:T(8,128)} %copy-done.7, f32[16,2048]{1,0:T(8,128)} %get-tuple-element.1005, f32[64]{0:T(128)S(1)} %get-tuple-element.1028, f32[16,2048]{1,0:T(8,128)} %copy-done, ...), kind=kLoop, calls=%fused_computation.35.clone.1 | loop fusion | flops 14548992 | bytes 34603520 | tf_op jit(solution)/shard_map/while/body/eval_jaxpr/reduce_sum | solution.py:79
  486.8 11.7 %copy.32 = f32[8,8,16,2048]{3,1,2,0:T(8,128)} copy(f32[8,8,16,2048]{3,2,1,0:T(8,128)} %bitcast.148) | data formatting | bytes 16777216 | tf_op jit(solution)/shard_map/while
  498.5 11.7 %copy.33 = f32[8,8,16,2048]{3,1,2,0:T(8,128)} copy(f32[8,8,16,2048]{3,2,1,0:T(8,128)} %bitcast.145) | data formatting | bytes 16777216 | tf_op jit(solution)/shard_map/while
  510.2 8.4 %copy.34 = f32[8,8,16,2048]{3,1,2,0:T(8,128)} copy(f32[8,8,16,2048]{3,2,1,0:T(8,128)S(1)} %bitcast.144) | data formatting | bytes 16777216 | tf_op jit(solution)/shard_map/while
  518.6 9.5 %fusion.56 = f32[32768]{0:T(1024)S(1)} fusion(f32[64,32768]{1,0:T(8,128)} %bitcast.149, f32[64,32768]{1,0:T(8,128)} %bitcast.150, f32[32768,64]{0,1:T(8,128)S(1)} %fusion.55, f32[64,32768]{1,0:T(8,128)} %bitcast.151, f32[32768]{0:T(1024)S(1)} %bitcast.153), kind=kLoop, calls=%fused_computation.31.clone.1 | loop fusion | flops 10452992 | bytes 33816576 | tf_op jit(solution)/shard_map/while/body/eval_jaxpr/reduce_sum | solution.py:78
  538.3 8.8 %fusion.55 = f32[32768,64]{0,1:T(8,128)S(1)} fusion(f32[64,32768]{1,0:T(8,128)S(1)} %bitcast.143), kind=kOutput, calls=%fused_computation.41.clone.1 | convolution fusion | flops 1610620928 | bytes 16777216 | tf_op jit(solution)/shard_map/while/body/eval_jaxpr/dot_general | solution.py:74
  547.1 8.0 %copy.31 = f32[8,8,16,2048]{3,2,1,0:T(8,128)} copy(f32[8,8,16,2048]{3,1,2,0:T(8,128)S(1)} %bitcast.140) | data formatting | bytes 16777216 | tf_op jit(solution)/shard_map/while
  555.1 10.9 %multiply_reduce_fusion.7 = (f32[64,2048]{1,0:T(8,128)S(1)}, f32[64,16,2048]{2,1,0:T(8,128)}, f32[64,16,2048]{2,1,0:T(8,128)S(1)}, f32[64,16,2048]{2,1,0:T(8,128)}) fusion(f32[16,2048]{1,0:T(8,128)} %copy-done.7, f32[16,2048]{1,0:T(8,128)} %get-tuple-element.1005, f32[64]{0:T(128)S(1)} %get-tuple-element.1028, f32[16,2048]{1,0:T(8,128)} %copy-done, ...), kind=kLoop, calls=%fused_computation.35.clone.1 | loop fusion | flops 14548992 | bytes 34603520 | tf_op jit(solution)/shard_map/while/body/eval_jaxpr/reduce_sum | solution.py:79
  571.9 11.7 %copy.32 = f32[8,8,16,2048]{3,1,2,0:T(8,128)} copy(f32[8,8,16,2048]{3,2,1,0:T(8,128)} %bitcast.148) | data formatting | bytes 16777216 | tf_op jit(solution)/shard_map/while
  583.5 11.7 %copy.33 = f32[8,8,16,2048]{3,1,2,0:T(8,128)} copy(f32[8,8,16,2048]{3,2,1,0:T(8,128)} %bitcast.145) | data formatting | bytes 16777216 | tf_op jit(solution)/shard_map/while
  595.2 8.2 %copy.34 = f32[8,8,16,2048]{3,1,2,0:T(8,128)} copy(f32[8,8,16,2048]{3,2,1,0:T(8,128)S(1)} %bitcast.144) | data formatting | bytes 16777216 | tf_op jit(solution)/shard_map/while
  603.4 9.5 %fusion.56 = f32[32768]{0:T(1024)S(1)} fusion(f32[64,32768]{1,0:T(8,128)} %bitcast.149, f32[64,32768]{1,0:T(8,128)} %bitcast.150, f32[32768,64]{0,1:T(8,128)S(1)} %fusion.55, f32[64,32768]{1,0:T(8,128)} %bitcast.151, f32[32768]{0:T(1024)S(1)} %bitcast.153), kind=kLoop, calls=%fused_computation.31.clone.1 | loop fusion | flops 10452992 | bytes 33816576 | tf_op jit(solution)/shard_map/while/body/eval_jaxpr/reduce_sum | solution.py:78
  618.2 13.6 %while.65 = (s32[]{:T(128)}, f32[16,2048]{1,0:T(8,128)}, s32[]{:T(128)}, f32[8,16,2048]{2,1,0:T(8,128)}, f32[8,16,2048]{2,1,0:T(8,128)}, /*index=5*/s32[]{:T(128)}, s32[]{:T(128)}) while((s32[]{:T(128)}, f32[16,2048]{1,0:T(8,128)}, s32[]{:T(128)}, f32[8,16,2048]{2,1,0:T(8,128)}, f32[8,16,2048]{2,1,0:T(8,128)}, ...), condition=%wide.region_4.5_spmd.clone, body=%wide.region_3.4_spmd.clone.sunk | while | flops 131076 | bytes 524397 | solution.py:22
  631.8 9.8 %all-gather.17.cloned.1.call-done = f32[128,2048]{1,0:T(8,128)} async-done(((f32[16,2048]{1,0:T(8,128)}), f32[128,2048]{1,0:T(8,128)}) %all-gather.17.cloned.1.call-update) | async-done | bytes 1048592 | tf_op jit(solution)/shard_map/all_gather | solution.py:9
  641.6 13.5 %while.66 = (s32[]{:T(128)}, f32[16,2048]{1,0:T(8,128)}, s32[]{:T(128)}, f32[8,16,2048]{2,1,0:T(8,128)}, f32[8,16,2048]{2,1,0:T(8,128)}, /*index=5*/s32[]{:T(128)}, s32[]{:T(128)}, s32[]{:T(128)}, s32[]{:T(128)}) while((s32[]{:T(128)}, f32[16,2048]{1,0:T(8,128)}, s32[]{:T(128)}, f32[8,16,2048]{2,1,0:T(8,128)}, ...), condition=%wide.region_11.12_spmd.clone, body=%wide.region_10.11_spmd.clone.sunk | while | flops 131080 | bytes 524459 | solution.py:22
  657.1 21.9 %multiply_reduce_fusion.2 = (f32[256,2048]{1,0:T(8,128)S(1)}, f32[256,2048]{1,0:T(8,128)S(1)}) fusion(f32[16,2048]{1,0:T(8,128)S(1)} %get-tuple-element.781, f32[256]{0:T(256)S(1)} %copy-done.20, f32[16,2048]{1,0:T(8,128)S(1)} %get-tuple-element.1121, f32[16,2048]{1,0:T(8,128)S(1)} %get-tuple-element.782, f32[256]{0:T(256)} %convert_add_fusion), kind=kLoop, calls=%fused_computation.44 | loop fusion | flops 49283072 | bytes 4589568 | tf_op jit(solution)/shard_map/reduce_sum | solution.py:99
  682.1 28.6 %all-reduce.2.cloned.1.call-done = f32[16,2048]{1,0:T(8,128)} async-done(((f32[16,2048]{1,0:T(8,128)}), f32[16,2048]{1,0:T(8,128)}) %all-reduce.2.cloned.1.call-update) | async-done | bytes 131088 | tf_op jit(solution)/shard_map/psum | solution.py:108
  (213 shorter events, 139.5 us)
Async XLA Ops:
  7.2 7.6 %copy-start.4 = (f32[16,2048]{1,0:T(8,128)S(1)}, f32[16,2048]{1,0:T(8,128)}, u32[]{:S(2)}) copy-start(f32[16,2048]{1,0:T(8,128)} %param.22) | copy-start | bytes 393220
  7.2 110.4 %all-gather.9.cloned.1.call-start = ((), (), s32[]{:S(2)}) async-start(), calls=%async_computation | async-start | bytes 5242880 | tf_op jit(solution)/shard_map/all_gather | solution.py:62
  7.9 246.2 %all-gather.11.cloned.1.call-start = ((), (), s32[]{:S(2)}) async-start(), calls=%async_computation.1 | async-start | bytes 37748736 | tf_op jit(solution)/shard_map/all_gather | solution.py:65
  8.7 609.5 %all-gather.13.cloned.1.call-start = ((), (), s32[]{:S(2)}) async-start(), calls=%async_computation.3 | async-start | bytes 1179648 | tf_op jit(solution)/shard_map/all_gather | solution.py:9
  10.5 607.8 %all-gather.15.cloned.1.call-start = ((), (), s32[]{:S(2)}) async-start(), calls=%async_computation.4 | async-start | bytes 1179648 | tf_op jit(solution)/shard_map/all_gather | solution.py:9
  116.3 525.3 %all-gather.17.cloned.1.call-start = ((), (), s32[]{:S(2)}) async-start(), calls=%async_computation.5 | async-start | bytes 1179648 | tf_op jit(solution)/shard_map/all_gather | solution.py:9
  274.3 382.7 %copy-start.20 = (f32[256]{0:T(256)S(1)}, f32[256]{0:T(256)}, u32[]{:S(2)}) copy-start(f32[256]{0:T(256)} %convert_subtract_fusion) | copy-start | bytes 3076
  274.5 4.2 copy-start
  274.5 4.2 copy-start.2
  274.5 4.2 copy-start.5
  274.5 4.2 copy-start.7
  340.4 8.2 %copy-start.9 = (f32[2,16,8,128]{3,1,2,0:T(8,128)S(1)}, f32[2,16,8,128]{3,1,2,0:T(8,128)}, u32[]{:S(2)}) copy-start(f32[2,16,8,128]{3,1,2,0:T(8,128)} %copy.35) | copy-start | bytes 393220 | tf_op jit(solution)/shard_map/while
  348.6 9.5 %copy-start.13 = (f32[16,2048]{1,0:T(8,128)S(1)}, f32[16,2048]{1,0:T(8,128)}, u32[]{:S(2)}) copy-start(f32[16,2048]{1,0:T(8,128)} %get-tuple-element.1006) | copy-start | bytes 393220 | tf_op jit(solution)/shard_map/while
  348.6 10.5 %copy-start.1 = (f32[16,2048]{1,0:T(8,128)S(1)}, f32[16,2048]{1,0:T(8,128)}, u32[]{:S(2)}) copy-start(f32[16,2048]{1,0:T(8,128)} %copy-done) | copy-start | bytes 393220 | tf_op jit(solution)/shard_map/while
  348.6 10.5 %copy-start.3 = (f32[4,64,2048]{2,1,0:T(8,128)S(1)}, f32[4,64,2048]{2,1,0:T(8,128)}, u32[]{:S(2)}) copy-start(f32[4,64,2048]{2,1,0:T(8,128)} %copy-done.2) | copy-start | bytes 6291460 | tf_op jit(solution)/shard_map/while
  348.6 10.5 %copy-start.6 = (f32[16,2048]{1,0:T(8,128)S(1)}, f32[16,2048]{1,0:T(8,128)}, u32[]{:S(2)}) copy-start(f32[16,2048]{1,0:T(8,128)} %copy-done.5) | copy-start | bytes 393220 | tf_op jit(solution)/shard_map/while
  348.6 10.5 %copy-start.8 = (f32[16,2048]{1,0:T(8,128)S(1)}, f32[16,2048]{1,0:T(8,128)}, u32[]{:S(2)}) copy-start(f32[16,2048]{1,0:T(8,128)} %copy-done.7) | copy-start | bytes 393220 | tf_op jit(solution)/shard_map/while
  359.4 4.2 copy-start
  359.4 4.2 copy-start.2
  425.3 8.2 %copy-start.9 = (f32[2,16,8,128]{3,1,2,0:T(8,128)S(1)}, f32[2,16,8,128]{3,1,2,0:T(8,128)}, u32[]{:S(2)}) copy-start(f32[2,16,8,128]{3,1,2,0:T(8,128)} %copy.35) | copy-start | bytes 393220 | tf_op jit(solution)/shard_map/while
  433.5 9.5 %copy-start.13 = (f32[16,2048]{1,0:T(8,128)S(1)}, f32[16,2048]{1,0:T(8,128)}, u32[]{:S(2)}) copy-start(f32[16,2048]{1,0:T(8,128)} %get-tuple-element.1006) | copy-start | bytes 393220 | tf_op jit(solution)/shard_map/while
  433.5 10.5 %copy-start.1 = (f32[16,2048]{1,0:T(8,128)S(1)}, f32[16,2048]{1,0:T(8,128)}, u32[]{:S(2)}) copy-start(f32[16,2048]{1,0:T(8,128)} %copy-done) | copy-start | bytes 393220 | tf_op jit(solution)/shard_map/while
  433.5 10.5 %copy-start.3 = (f32[4,64,2048]{2,1,0:T(8,128)S(1)}, f32[4,64,2048]{2,1,0:T(8,128)}, u32[]{:S(2)}) copy-start(f32[4,64,2048]{2,1,0:T(8,128)} %copy-done.2) | copy-start | bytes 6291460 | tf_op jit(solution)/shard_map/while
  433.5 10.5 %copy-start.6 = (f32[16,2048]{1,0:T(8,128)S(1)}, f32[16,2048]{1,0:T(8,128)}, u32[]{:S(2)}) copy-start(f32[16,2048]{1,0:T(8,128)} %copy-done.5) | copy-start | bytes 393220 | tf_op jit(solution)/shard_map/while
  433.5 10.5 %copy-start.8 = (f32[16,2048]{1,0:T(8,128)S(1)}, f32[16,2048]{1,0:T(8,128)}, u32[]{:S(2)}) copy-start(f32[16,2048]{1,0:T(8,128)} %copy-done.7) | copy-start | bytes 393220 | tf_op jit(solution)/shard_map/while
  510.2 8.4 %copy-start.9 = (f32[2,16,8,128]{3,1,2,0:T(8,128)S(1)}, f32[2,16,8,128]{3,1,2,0:T(8,128)}, u32[]{:S(2)}) copy-start(f32[2,16,8,128]{3,1,2,0:T(8,128)} %copy.35) | copy-start | bytes 393220 | tf_op jit(solution)/shard_map/while
  518.6 9.5 %copy-start.13 = (f32[16,2048]{1,0:T(8,128)S(1)}, f32[16,2048]{1,0:T(8,128)}, u32[]{:S(2)}) copy-start(f32[16,2048]{1,0:T(8,128)} %get-tuple-element.1006) | copy-start | bytes 393220 | tf_op jit(solution)/shard_map/while
  518.6 10.4 %copy-start.1 = (f32[16,2048]{1,0:T(8,128)S(1)}, f32[16,2048]{1,0:T(8,128)}, u32[]{:S(2)}) copy-start(f32[16,2048]{1,0:T(8,128)} %copy-done) | copy-start | bytes 393220 | tf_op jit(solution)/shard_map/while
  518.6 10.4 %copy-start.3 = (f32[4,64,2048]{2,1,0:T(8,128)S(1)}, f32[4,64,2048]{2,1,0:T(8,128)}, u32[]{:S(2)}) copy-start(f32[4,64,2048]{2,1,0:T(8,128)} %copy-done.2) | copy-start | bytes 6291460 | tf_op jit(solution)/shard_map/while
  518.6 10.4 %copy-start.6 = (f32[16,2048]{1,0:T(8,128)S(1)}, f32[16,2048]{1,0:T(8,128)}, u32[]{:S(2)}) copy-start(f32[16,2048]{1,0:T(8,128)} %copy-done.5) | copy-start | bytes 393220 | tf_op jit(solution)/shard_map/while
  518.6 10.4 %copy-start.8 = (f32[16,2048]{1,0:T(8,128)S(1)}, f32[16,2048]{1,0:T(8,128)}, u32[]{:S(2)}) copy-start(f32[16,2048]{1,0:T(8,128)} %copy-done.7) | copy-start | bytes 393220 | tf_op jit(solution)/shard_map/while
  529.2 4.2 copy-start
  529.2 4.2 copy-start.2
  529.3 4.2 copy-start.5
  529.3 4.2 copy-start.7
  595.2 8.2 %copy-start.9 = (f32[2,16,8,128]{3,1,2,0:T(8,128)S(1)}, f32[2,16,8,128]{3,1,2,0:T(8,128)}, u32[]{:S(2)}) copy-start(f32[2,16,8,128]{3,1,2,0:T(8,128)} %copy.35) | copy-start | bytes 393220 | tf_op jit(solution)/shard_map/while
  603.4 9.5 %copy-start.13 = (f32[16,2048]{1,0:T(8,128)S(1)}, f32[16,2048]{1,0:T(8,128)}, u32[]{:S(2)}) copy-start(f32[16,2048]{1,0:T(8,128)} %get-tuple-element.1006) | copy-start | bytes 393220 | tf_op jit(solution)/shard_map/while
  603.4 10.5 %copy-start.1 = (f32[16,2048]{1,0:T(8,128)S(1)}, f32[16,2048]{1,0:T(8,128)}, u32[]{:S(2)}) copy-start(f32[16,2048]{1,0:T(8,128)} %copy-done) | copy-start | bytes 393220 | tf_op jit(solution)/shard_map/while
  603.4 10.5 %copy-start.3 = (f32[4,64,2048]{2,1,0:T(8,128)S(1)}, f32[4,64,2048]{2,1,0:T(8,128)}, u32[]{:S(2)}) copy-start(f32[4,64,2048]{2,1,0:T(8,128)} %copy-done.2) | copy-start | bytes 6291460 | tf_op jit(solution)/shard_map/while
  603.4 10.5 %copy-start.6 = (f32[16,2048]{1,0:T(8,128)S(1)}, f32[16,2048]{1,0:T(8,128)}, u32[]{:S(2)}) copy-start(f32[16,2048]{1,0:T(8,128)} %copy-done.5) | copy-start | bytes 393220 | tf_op jit(solution)/shard_map/while
  603.4 10.5 %copy-start.8 = (f32[16,2048]{1,0:T(8,128)S(1)}, f32[16,2048]{1,0:T(8,128)}, u32[]{:S(2)}) copy-start(f32[16,2048]{1,0:T(8,128)} %copy-done.7) | copy-start | bytes 393220 | tf_op jit(solution)/shard_map/while
  618.1 92.5 %all-reduce.2.cloned.1.call-start = ((), (), s32[]{:S(2)}) async-start(), calls=%async_computation.2 | async-start | bytes 262144 | tf_op jit(solution)/shard_map/psum | solution.py:108
  657.0 22.0 %copy-start.11 = (f32[4,64,2048]{2,1,0:T(8,128)S(1)}, f32[4,64,2048]{2,1,0:T(8,128)}, u32[]{:S(2)}) copy-start(f32[4,64,2048]{2,1,0:T(8,128)} %get-tuple-element.500) | copy-start | bytes 6291460
  657.0 22.0 %copy-start.12 = (f32[4,64,2048]{2,1,0:T(8,128)S(1)}, f32[4,64,2048]{2,1,0:T(8,128)}, u32[]{:S(2)}) copy-start(f32[4,64,2048]{2,1,0:T(8,128)} %get-tuple-element.497) | copy-start | bytes 6291460
  657.1 22.0 %copy-start.15 = (bf16[256,2048]{1,0:T(8,128)(2,1)S(1)}, bf16[256,2048]{1,0:T(8,128)(2,1)}, u32[]{:S(2)}) copy-start(bf16[256,2048]{1,0:T(8,128)(2,1)} %param.17) | copy-start | bytes 3145732
  657.1 22.0 %copy-start.16 = (bf16[256,2048]{1,0:T(8,128)(2,1)S(1)}, bf16[256,2048]{1,0:T(8,128)(2,1)}, u32[]{:S(2)}) copy-start(bf16[256,2048]{1,0:T(8,128)(2,1)} %param.18) | copy-start | bytes 3145732
  657.1 22.0 %copy-start.17 = (f32[256,2048]{1,0:T(8,128)S(1)}, f32[256,2048]{1,0:T(8,128)}, u32[]{:S(2)}) copy-start(f32[256,2048]{1,0:T(8,128)} %get-tuple-element.788) | copy-start | bytes 6291460
  657.1 22.0 %copy-start.19 = (f32[256]{0:T(256)S(1)}, f32[256]{0:T(256)}, u32[]{:S(2)}) copy-start(f32[256]{0:T(256)} %copy-done.18) | copy-start | bytes 3076
  (12 other events, 31.5 us)
Sparse Core Ops, SparseCore 0:
  9.6 83.4 all-gather.8
  94.9 159.1 all-gather.10
  256.6 23.3 all-gather.12
  282.3 23.3 all-gather.14
  618.2 23.3 all-gather.16
  657.1 53.4 all-reduce.1
where the time goes:
time: 721 us; the launch traced here: 719 us
  local copies, waits for them, and re-layouts  266 us (37%)
  waiting for transfers between devices  176 us (24%)
  other arithmetic  169 us (23%)
  matrix products  87.4 us (12%)
  between operations  14.7 us (2%)
    while x120, local copies, waits for them, and re-layouts  225 us
    all_gather x1, waiting for transfers between devices, body(): lax.all_gather(out_weight, 'ctx', axis=0, tiled=True)  137 us
    reduce_sum x4, other arithmetic, backward_block(): return ((states[0], running), jnp.sum(filter_gain[None] * states, axis=1))  43.2 us
    reduce_sum x4, other arithmetic, backward_block(): running = running + jnp.sum(input_blk[:, None, :] * states, axis=0)  37.9 us
    dot_general x4, matrix products, backward_block(): jnp.dot(upper_ones, scaled, precision=lax.Precision.HIGHEST)  35.5 us
    dot_general x4, matrix products, forward_block(): jnp.dot(lower_ones, scaled, precision=lax.Precision.HIGHEST)  34 us
    psum x1, waiting for transfers between devices, body(): filter_grad = lax.psum(filter_terms, 'ctx')  28.6 us
    select_n x16, other arithmetic, turn(): return jax.tree.map(lambda a, b: jnp.where(reached, a, b), new, before)  27.1 us
  transfers between devices with their start and end apart: 6, of which 3 were waited for; matrix products, arithmetic and copies ran while one was open for 70% of the time, Pallas kernels for 0%

commit v1 on v0

--- a/solution.py
+++ b/solution.py
@@ -105,7 +105,10 @@
     key_grad = (live * input_grad * value_act.astype(jnp.float32)).astype(jnp.bfloat16)
     value_grad = (live * input_grad * key_act.astype(jnp.float32)).astype(jnp.bfloat16)
     filter_terms = root_gain * (filter_local + backward_in * step_decay * end_state)
-    filter_grad = lax.psum(filter_terms, "ctx")
+    count, filter_grad = (lax.axis_size("ctx"), filter_terms)
+    for reach in [1 << k_2 for k_2 in range(count.bit_length() - 1)]:
+        route = [(i, i ^ reach) for i in range(count)]
+        filter_grad = filter_grad + lax.ppermute(filter_grad, "ctx", route)
     return (query_grad, key_grad, value_grad, filter_grad)
 
 

time: 721 us -> 694 us (0.963)
  waiting for transfers between devices: 176 us -> 152 us
    psum x1 -> x0, waiting for transfers between devices: 28.6 us -> none  [body(): filter_grad = lax.psum(filter_terms, 'ctx')]
  transfers between devices with their start and end apart: 6 -> 8, of which waited for: 3 -> 4; matrix products, arithmetic and copies ran while one was open for 70% -> 72% of each run, Pallas kernels for 0% -> 0%
where the time goes in v1:
time: 694 us; the launch traced here: 693 us
  local copies, waits for them, and re-layouts  264 us (38%)
  other arithmetic  166 us (24%)
  waiting for transfers between devices  152 us (22%)
  matrix products  87.4 us (13%)
  between operations  14.3 us (2%)
    while x120, local copies, waits for them, and re-layouts  224 us
    all_gather x1, waiting for transfers between devices, body(): lax.all_gather(out_weight, 'ctx', axis=0, tiled=True)  138 us
    reduce_sum x4, other arithmetic, backward_block(): return ((states[0], running), jnp.sum(filter_gain[None] * states, axis=1))  43.2 us
    reduce_sum x4, other arithmetic, backward_block(): running = running + jnp.sum(input_blk[:, None, :] * states, axis=0)  37.9 us
    dot_general x4, matrix products, backward_block(): jnp.dot(upper_ones, scaled, precision=lax.Precision.HIGHEST)  35.5 us
    dot_general x4, matrix products, forward_block(): jnp.dot(lower_ones, scaled, precision=lax.Precision.HIGHEST)  34 us
    select_n x16, other arithmetic, turn(): return jax.tree.map(lambda a, b: jnp.where(reached, a, b), new, before)  27 us
    mul x8, local copies, waits for them, and re-layouts, backward_block(): running = running + jnp.sum(input_blk[:, None, :] * states, axis=0)  21.7 us
  transfers between devices with their start and end apart: 8, of which 4 were waited for; matrix products, arithmetic and copies ran while one was open for 72% of the time, Pallas kernels for 0%

profile of v1, /device:TPU:0, one launch (start us, length us, event | category | flops | bytes accessed | tf_op | source)
XLA Modules:
  0.0 692.9 jit_solution(50258437680005624)
XLA Ops:
  14.7 100.9 %while.67 = (s32[]{:T(128)}, f32[16,2048]{1,0:T(8,128)S(1)}, f32[4,64,2048]{2,1,0:T(8,128)}, f32[4,64,2048]{2,1,0:T(8,128)S(1)}, f32[16,2048]{1,0:T(8,128)S(1)},...) while((s32[]{:T(128)}, f32[16,2048]{1,0:T(8,128)S(1)}, ...), condition=%wide.region_2.3_spmd.clone.clone, body=%wide.region_0.2_spmd.clone.clone.sunk | while | flops 1629364224 | bytes 79561336 | solution.py:58
  16.1 5.0 copy.28
  21.2 8.5 %fusion.52 = f32[32768,64]{0,1:T(8,128)S(1)} fusion(f32[64,32768]{1,0:T(8,128)S(1)} %bitcast.141), kind=kOutput, calls=%fused_computation.23.clone.1 | convolution fusion | flops 1610620928 | bytes 16777216 | tf_op jit(solution)/shard_map/while/body/eval_jaxpr/dot_general | solution.py:52
  29.7 5.0 copy.29
  41.3 5.0 copy.28
  46.3 8.5 %fusion.52 = f32[32768,64]{0,1:T(8,128)S(1)} fusion(f32[64,32768]{1,0:T(8,128)S(1)} %bitcast.141), kind=kOutput, calls=%fused_computation.23.clone.1 | convolution fusion | flops 1610620928 | bytes 16777216 | tf_op jit(solution)/shard_map/while/body/eval_jaxpr/dot_general | solution.py:52
  54.8 5.0 copy.29
  66.4 5.0 copy.28
  71.4 8.5 %fusion.52 = f32[32768,64]{0,1:T(8,128)S(1)} fusion(f32[64,32768]{1,0:T(8,128)S(1)} %bitcast.141), kind=kOutput, calls=%fused_computation.23.clone.1 | convolution fusion | flops 1610620928 | bytes 16777216 | tf_op jit(solution)/shard_map/while/body/eval_jaxpr/dot_general | solution.py:52
  80.0 5.0 copy.29
  91.6 5.0 copy.28
  96.6 8.5 %fusion.52 = f32[32768,64]{0,1:T(8,128)S(1)} fusion(f32[64,32768]{1,0:T(8,128)S(1)} %bitcast.141), kind=kOutput, calls=%fused_computation.23.clone.1 | convolution fusion | flops 1610620928 | bytes 16777216 | tf_op jit(solution)/shard_map/while/body/eval_jaxpr/dot_general | solution.py:52
  105.1 5.0 copy.29
  116.5 137.7 %all-gather.11.cloned.1.call-done = bf16[8192,2048]{1,0:T(8,128)(2,1)} async-done(((bf16[1024,2048]{1,0:T(8,128)(2,1)}), bf16[8192,2048]{1,0:T(8,128)(2,1)}) %all-gather.11.cloned.1.call-update) | async-done | bytes 33554448 | tf_op jit(solution)/shard_map/all_gather | solution.py:65
  254.1 17.9 %convert_multiply_fusion.4 = (f32[256,2048]{1,0:T(8,128)}, f32[256,2048]{1,0:T(8,128)}) fusion(bf16[256,2048]{1,0:T(8,128)(2,1)} %param.16, bf16[256,8192]{1,0:T(8,128)(2,1)} %all-gather.9.cloned.1.call-done, bf16[8192,2048]{1,0:T(8,128)(2,1)} %all-gather.11.cloned.1.call-done), kind=kOutput, calls=%fused_computation.57 | convolution fusion | flops 8590983168 | bytes 42991616 | tf_op jit(solution)/shard_map/dot_general | solution.py:63
  274.3 343.8 %while.68 = (s32[]{:T(128)}, f32[16,2048]{1,0:T(8,128)}, f32[16,2048]{1,0:T(8,128)}, f32[4,64,2048]{2,1,0:T(8,128)}, f32[4,64,2048]{2,1,0:T(8,128)}, /*index=5*/...) while((s32[]{:T(128)}, f32[16,2048]{1,0:T(8,128)}, ...), condition=%wide.region_9.10_spmd.clone.clone.clone, body=%wide.region_6.0_spmd.clone.clone.clone.sunk | while | flops 1639882752 | bytes 212862208 | solution.py:81
  283.5 8.8 %fusion.55 = f32[32768,64]{0,1:T(8,128)S(1)} fusion(f32[64,32768]{1,0:T(8,128)S(1)} %bitcast.143), kind=kOutput, calls=%fused_computation.41.clone.1 | convolution fusion | flops 1610620928 | bytes 16777216 | tf_op jit(solution)/shard_map/while/body/eval_jaxpr/dot_general | solution.py:74
  292.3 8.0 %copy.31 = f32[8,8,16,2048]{3,2,1,0:T(8,128)} copy(f32[8,8,16,2048]{3,1,2,0:T(8,128)S(1)} %bitcast.140) | data formatting | bytes 16777216 | tf_op jit(solution)/shard_map/while
  300.3 10.9 %multiply_reduce_fusion.7 = (f32[64,2048]{1,0:T(8,128)S(1)}, f32[64,16,2048]{2,1,0:T(8,128)}, f32[64,16,2048]{2,1,0:T(8,128)S(1)}, f32[64,16,2048]{2,1,0:T(8,128)}) fusion(f32[16,2048]{1,0:T(8,128)} %copy-done.7, f32[16,2048]{1,0:T(8,128)} %get-tuple-element.1005, f32[64]{0:T(128)S(1)} %get-tuple-element.1028, f32[16,2048]{1,0:T(8,128)} %copy-done, ...), kind=kLoop, calls=%fused_computation.35.clone.1 | loop fusion | flops 14548992 | bytes 34603520 | tf_op jit(solution)/shard_map/while/body/eval_jaxpr/reduce_sum | solution.py:79
  317.1 11.7 %copy.32 = f32[8,8,16,2048]{3,1,2,0:T(8,128)} copy(f32[8,8,16,2048]{3,2,1,0:T(8,128)} %bitcast.148) | data formatting | bytes 16777216 | tf_op jit(solution)/shard_map/while
  328.8 11.7 %copy.33 = f32[8,8,16,2048]{3,1,2,0:T(8,128)} copy(f32[8,8,16,2048]{3,2,1,0:T(8,128)} %bitcast.145) | data formatting | bytes 16777216 | tf_op jit(solution)/shard_map/while
  340.5 8.2 %copy.34 = f32[8,8,16,2048]{3,1,2,0:T(8,128)} copy(f32[8,8,16,2048]{3,2,1,0:T(8,128)S(1)} %bitcast.144) | data formatting | bytes 16777216 | tf_op jit(solution)/shard_map/while
  348.7 9.5 %fusion.56 = f32[32768]{0:T(1024)S(1)} fusion(f32[64,32768]{1,0:T(8,128)} %bitcast.149, f32[64,32768]{1,0:T(8,128)} %bitcast.150, f32[32768,64]{0,1:T(8,128)S(1)} %fusion.55, f32[64,32768]{1,0:T(8,128)} %bitcast.151, f32[32768]{0:T(1024)S(1)} %bitcast.153), kind=kLoop, calls=%fused_computation.31.clone.1 | loop fusion | flops 10452992 | bytes 33816576 | tf_op jit(solution)/shard_map/while/body/eval_jaxpr/reduce_sum | solution.py:78
  368.4 9.0 %fusion.55 = f32[32768,64]{0,1:T(8,128)S(1)} fusion(f32[64,32768]{1,0:T(8,128)S(1)} %bitcast.143), kind=kOutput, calls=%fused_computation.41.clone.1 | convolution fusion | flops 1610620928 | bytes 16777216 | tf_op jit(solution)/shard_map/while/body/eval_jaxpr/dot_general | solution.py:74
  377.4 8.0 %copy.31 = f32[8,8,16,2048]{3,2,1,0:T(8,128)} copy(f32[8,8,16,2048]{3,1,2,0:T(8,128)S(1)} %bitcast.140) | data formatting | bytes 16777216 | tf_op jit(solution)/shard_map/while
  385.4 10.7 %multiply_reduce_fusion.7 = (f32[64,2048]{1,0:T(8,128)S(1)}, f32[64,16,2048]{2,1,0:T(8,128)}, f32[64,16,2048]{2,1,0:T(8,128)S(1)}, f32[64,16,2048]{2,1,0:T(8,128)}) fusion(f32[16,2048]{1,0:T(8,128)} %copy-done.7, f32[16,2048]{1,0:T(8,128)} %get-tuple-element.1005, f32[64]{0:T(128)S(1)} %get-tuple-element.1028, f32[16,2048]{1,0:T(8,128)} %copy-done, ...), kind=kLoop, calls=%fused_computation.35.clone.1 | loop fusion | flops 14548992 | bytes 34603520 | tf_op jit(solution)/shard_map/while/body/eval_jaxpr/reduce_sum | solution.py:79
  401.9 11.7 %copy.32 = f32[8,8,16,2048]{3,1,2,0:T(8,128)} copy(f32[8,8,16,2048]{3,2,1,0:T(8,128)} %bitcast.148) | data formatting | bytes 16777216 | tf_op jit(solution)/shard_map/while
  413.6 11.7 %copy.33 = f32[8,8,16,2048]{3,1,2,0:T(8,128)} copy(f32[8,8,16,2048]{3,2,1,0:T(8,128)} %bitcast.145) | data formatting | bytes 16777216 | tf_op jit(solution)/shard_map/while
  425.3 8.2 %copy.34 = f32[8,8,16,2048]{3,1,2,0:T(8,128)} copy(f32[8,8,16,2048]{3,2,1,0:T(8,128)S(1)} %bitcast.144) | data formatting | bytes 16777216 | tf_op jit(solution)/shard_map/while
  433.5 9.5 %fusion.56 = f32[32768]{0:T(1024)S(1)} fusion(f32[64,32768]{1,0:T(8,128)} %bitcast.149, f32[64,32768]{1,0:T(8,128)} %bitcast.150, f32[32768,64]{0,1:T(8,128)S(1)} %fusion.55, f32[64,32768]{1,0:T(8,128)} %bitcast.151, f32[32768]{0:T(1024)S(1)} %bitcast.153), kind=kLoop, calls=%fused_computation.31.clone.1 | loop fusion | flops 10452992 | bytes 33816576 | tf_op jit(solution)/shard_map/while/body/eval_jaxpr/reduce_sum | solution.py:78
  453.4 8.8 %fusion.55 = f32[32768,64]{0,1:T(8,128)S(1)} fusion(f32[64,32768]{1,0:T(8,128)S(1)} %bitcast.143), kind=kOutput, calls=%fused_computation.41.clone.1 | convolution fusion | flops 1610620928 | bytes 16777216 | tf_op jit(solution)/shard_map/while/body/eval_jaxpr/dot_general | solution.py:74
  462.2 8.0 %copy.31 = f32[8,8,16,2048]{3,2,1,0:T(8,128)} copy(f32[8,8,16,2048]{3,1,2,0:T(8,128)S(1)} %bitcast.140) | data formatting | bytes 16777216 | tf_op jit(solution)/shard_map/while
  470.2 10.7 %multiply_reduce_fusion.7 = (f32[64,2048]{1,0:T(8,128)S(1)}, f32[64,16,2048]{2,1,0:T(8,128)}, f32[64,16,2048]{2,1,0:T(8,128)S(1)}, f32[64,16,2048]{2,1,0:T(8,128)}) fusion(f32[16,2048]{1,0:T(8,128)} %copy-done.7, f32[16,2048]{1,0:T(8,128)} %get-tuple-element.1005, f32[64]{0:T(128)S(1)} %get-tuple-element.1028, f32[16,2048]{1,0:T(8,128)} %copy-done, ...), kind=kLoop, calls=%fused_computation.35.clone.1 | loop fusion | flops 14548992 | bytes 34603520 | tf_op jit(solution)/shard_map/while/body/eval_jaxpr/reduce_sum | solution.py:79
  486.8 11.7 %copy.32 = f32[8,8,16,2048]{3,1,2,0:T(8,128)} copy(f32[8,8,16,2048]{3,2,1,0:T(8,128)} %bitcast.148) | data formatting | bytes 16777216 | tf_op jit(solution)/shard_map/while
  498.4 11.7 %copy.33 = f32[8,8,16,2048]{3,1,2,0:T(8,128)} copy(f32[8,8,16,2048]{3,2,1,0:T(8,128)} %bitcast.145) | data formatting | bytes 16777216 | tf_op jit(solution)/shard_map/while
  510.1 8.4 %copy.34 = f32[8,8,16,2048]{3,1,2,0:T(8,128)} copy(f32[8,8,16,2048]{3,2,1,0:T(8,128)S(1)} %bitcast.144) | data formatting | bytes 16777216 | tf_op jit(solution)/shard_map/while
  518.6 9.5 %fusion.56 = f32[32768]{0:T(1024)S(1)} fusion(f32[64,32768]{1,0:T(8,128)} %bitcast.149, f32[64,32768]{1,0:T(8,128)} %bitcast.150, f32[32768,64]{0,1:T(8,128)S(1)} %fusion.55, f32[64,32768]{1,0:T(8,128)} %bitcast.151, f32[32768]{0:T(1024)S(1)} %bitcast.153), kind=kLoop, calls=%fused_computation.31.clone.1 | loop fusion | flops 10452992 | bytes 33816576 | tf_op jit(solution)/shard_map/while/body/eval_jaxpr/reduce_sum | solution.py:78
  538.2 8.8 %fusion.55 = f32[32768,64]{0,1:T(8,128)S(1)} fusion(f32[64,32768]{1,0:T(8,128)S(1)} %bitcast.143), kind=kOutput, calls=%fused_computation.41.clone.1 | convolution fusion | flops 1610620928 | bytes 16777216 | tf_op jit(solution)/shard_map/while/body/eval_jaxpr/dot_general | solution.py:74
  547.0 8.0 %copy.31 = f32[8,8,16,2048]{3,2,1,0:T(8,128)} copy(f32[8,8,16,2048]{3,1,2,0:T(8,128)S(1)} %bitcast.140) | data formatting | bytes 16777216 | tf_op jit(solution)/shard_map/while
  555.0 10.9 %multiply_reduce_fusion.7 = (f32[64,2048]{1,0:T(8,128)S(1)}, f32[64,16,2048]{2,1,0:T(8,128)}, f32[64,16,2048]{2,1,0:T(8,128)S(1)}, f32[64,16,2048]{2,1,0:T(8,128)}) fusion(f32[16,2048]{1,0:T(8,128)} %copy-done.7, f32[16,2048]{1,0:T(8,128)} %get-tuple-element.1005, f32[64]{0:T(128)S(1)} %get-tuple-element.1028, f32[16,2048]{1,0:T(8,128)} %copy-done, ...), kind=kLoop, calls=%fused_computation.35.clone.1 | loop fusion | flops 14548992 | bytes 34603520 | tf_op jit(solution)/shard_map/while/body/eval_jaxpr/reduce_sum | solution.py:79
  571.8 11.7 %copy.32 = f32[8,8,16,2048]{3,1,2,0:T(8,128)} copy(f32[8,8,16,2048]{3,2,1,0:T(8,128)} %bitcast.148) | data formatting | bytes 16777216 | tf_op jit(solution)/shard_map/while
  583.5 11.7 %copy.33 = f32[8,8,16,2048]{3,1,2,0:T(8,128)} copy(f32[8,8,16,2048]{3,2,1,0:T(8,128)} %bitcast.145) | data formatting | bytes 16777216 | tf_op jit(solution)/shard_map/while
  595.2 8.2 %copy.34 = f32[8,8,16,2048]{3,1,2,0:T(8,128)} copy(f32[8,8,16,2048]{3,2,1,0:T(8,128)S(1)} %bitcast.144) | data formatting | bytes 16777216 | tf_op jit(solution)/shard_map/while
  603.4 9.5 %fusion.56 = f32[32768]{0:T(1024)S(1)} fusion(f32[64,32768]{1,0:T(8,128)} %bitcast.149, f32[64,32768]{1,0:T(8,128)} %bitcast.150, f32[32768,64]{0,1:T(8,128)S(1)} %fusion.55, f32[64,32768]{1,0:T(8,128)} %bitcast.151, f32[32768]{0:T(1024)S(1)} %bitcast.153), kind=kLoop, calls=%fused_computation.31.clone.1 | loop fusion | flops 10452992 | bytes 33816576 | tf_op jit(solution)/shard_map/while/body/eval_jaxpr/reduce_sum | solution.py:78
  618.2 13.5 %while.65 = (s32[]{:T(128)}, f32[16,2048]{1,0:T(8,128)}, s32[]{:T(128)}, f32[8,16,2048]{2,1,0:T(8,128)}, f32[8,16,2048]{2,1,0:T(8,128)}, /*index=5*/s32[]{:T(128)}, s32[]{:T(128)}) while((s32[]{:T(128)}, f32[16,2048]{1,0:T(8,128)}, s32[]{:T(128)}, f32[8,16,2048]{2,1,0:T(8,128)}, f32[8,16,2048]{2,1,0:T(8,128)}, ...), condition=%wide.region_4.5_spmd.clone, body=%wide.region_3.4_spmd.clone.sunk | while | flops 131076 | bytes 524397 | solution.py:22
  631.7 9.9 %all-gather.17.cloned.1.call-done = f32[128,2048]{1,0:T(8,128)} async-done(((f32[16,2048]{1,0:T(8,128)}), f32[128,2048]{1,0:T(8,128)}) %all-gather.17.cloned.1.call-update) | async-done | bytes 1048592 | tf_op jit(solution)/shard_map/all_gather | solution.py:9
  641.7 13.5 %while.66 = (s32[]{:T(128)}, f32[16,2048]{1,0:T(8,128)}, s32[]{:T(128)}, f32[8,16,2048]{2,1,0:T(8,128)}, f32[8,16,2048]{2,1,0:T(8,128)}, /*index=5*/s32[]{:T(128)}, s32[]{:T(128)}, s32[]{:T(128)}, s32[]{:T(128)}) while((s32[]{:T(128)}, f32[16,2048]{1,0:T(8,128)}, s32[]{:T(128)}, f32[8,16,2048]{2,1,0:T(8,128)}, ...), condition=%wide.region_11.12_spmd.clone, body=%wide.region_10.11_spmd.clone.sunk | while | flops 131080 | bytes 524459 | solution.py:22
  659.4 20.5 %multiply_reduce_fusion.2 = (f32[256,2048]{1,0:T(8,128)S(1)}, f32[256,2048]{1,0:T(8,128)S(1)}) fusion(f32[16,2048]{1,0:T(8,128)S(1)} %get-tuple-element.781, f32[256]{0:T(256)S(1)} %convert_subtract_fusion, f32[16,2048]{1,0:T(8,128)S(1)} %get-tuple-element.1116, f32[16,2048]{1,0:T(8,128)S(1)} %get-tuple-element.782, f32[256]{0:T(256)S(1)} %convert_add_fusion), kind=kLoop, calls=%fused_computation.44 | loop fusion | flops 49283072 | bytes 4589568 | tf_op jit(solution)/shard_map/reduce_sum | solution.py:99
  (216 shorter events, 136.9 us)
Async XLA Ops:
  7.2 7.5 %copy-start.4 = (f32[16,2048]{1,0:T(8,128)S(1)}, f32[16,2048]{1,0:T(8,128)}, u32[]{:S(2)}) copy-start(f32[16,2048]{1,0:T(8,128)} %param.22) | copy-start | bytes 393220
  7.2 109.3 %all-gather.9.cloned.1.call-start = ((), (), s32[]{:S(2)}) async-start(), calls=%async_computation | async-start | bytes 5242880 | tf_op jit(solution)/shard_map/all_gather | solution.py:62
  7.9 246.2 %all-gather.11.cloned.1.call-start = ((), (), s32[]{:S(2)}) async-start(), calls=%async_computation.1 | async-start | bytes 37748736 | tf_op jit(solution)/shard_map/all_gather | solution.py:65
  8.7 609.5 %all-gather.13.cloned.1.call-start = ((), (), s32[]{:S(2)}) async-start(), calls=%async_computation.2 | async-start | bytes 1179648 | tf_op jit(solution)/shard_map/all_gather | solution.py:9
  10.5 607.7 %all-gather.15.cloned.1.call-start = ((), (), s32[]{:S(2)}) async-start(), calls=%async_computation.3 | async-start | bytes 1179648 | tf_op jit(solution)/shard_map/all_gather | solution.py:9
  116.3 525.4 %all-gather.17.cloned.1.call-start = ((), (), s32[]{:S(2)}) async-start(), calls=%async_computation.4 | async-start | bytes 1179648 | tf_op jit(solution)/shard_map/all_gather | solution.py:9
  274.5 4.2 copy-start
  274.5 4.2 copy-start.2
  274.5 4.2 copy-start.5
  274.5 4.2 copy-start.7
  340.5 8.2 %copy-start.9 = (f32[2,16,8,128]{3,1,2,0:T(8,128)S(1)}, f32[2,16,8,128]{3,1,2,0:T(8,128)}, u32[]{:S(2)}) copy-start(f32[2,16,8,128]{3,1,2,0:T(8,128)} %copy.35) | copy-start | bytes 393220 | tf_op jit(solution)/shard_map/while
  348.6 9.5 %copy-start.13 = (f32[16,2048]{1,0:T(8,128)S(1)}, f32[16,2048]{1,0:T(8,128)}, u32[]{:S(2)}) copy-start(f32[16,2048]{1,0:T(8,128)} %get-tuple-element.1006) | copy-start | bytes 393220 | tf_op jit(solution)/shard_map/while
  348.6 10.5 %copy-start.1 = (f32[16,2048]{1,0:T(8,128)S(1)}, f32[16,2048]{1,0:T(8,128)}, u32[]{:S(2)}) copy-start(f32[16,2048]{1,0:T(8,128)} %copy-done) | copy-start | bytes 393220 | tf_op jit(solution)/shard_map/while
  348.6 10.5 %copy-start.3 = (f32[4,64,2048]{2,1,0:T(8,128)S(1)}, f32[4,64,2048]{2,1,0:T(8,128)}, u32[]{:S(2)}) copy-start(f32[4,64,2048]{2,1,0:T(8,128)} %copy-done.2) | copy-start | bytes 6291460 | tf_op jit(solution)/shard_map/while
  348.6 10.5 %copy-start.6 = (f32[16,2048]{1,0:T(8,128)S(1)}, f32[16,2048]{1,0:T(8,128)}, u32[]{:S(2)}) copy-start(f32[16,2048]{1,0:T(8,128)} %copy-done.5) | copy-start | bytes 393220 | tf_op jit(solution)/shard_map/while
  348.6 10.5 %copy-start.8 = (f32[16,2048]{1,0:T(8,128)S(1)}, f32[16,2048]{1,0:T(8,128)}, u32[]{:S(2)}) copy-start(f32[16,2048]{1,0:T(8,128)} %copy-done.7) | copy-start | bytes 393220 | tf_op jit(solution)/shard_map/while
  359.4 4.2 copy-start
  359.4 4.2 copy-start.2
  359.4 4.2 copy-start.5
  359.4 4.2 copy-start.7
  425.3 8.2 %copy-start.9 = (f32[2,16,8,128]{3,1,2,0:T(8,128)S(1)}, f32[2,16,8,128]{3,1,2,0:T(8,128)}, u32[]{:S(2)}) copy-start(f32[2,16,8,128]{3,1,2,0:T(8,128)} %copy.35) | copy-start | bytes 393220 | tf_op jit(solution)/shard_map/while
  433.5 9.5 %copy-start.13 = (f32[16,2048]{1,0:T(8,128)S(1)}, f32[16,2048]{1,0:T(8,128)}, u32[]{:S(2)}) copy-start(f32[16,2048]{1,0:T(8,128)} %get-tuple-element.1006) | copy-start | bytes 393220 | tf_op jit(solution)/shard_map/while
  433.5 10.5 %copy-start.1 = (f32[16,2048]{1,0:T(8,128)S(1)}, f32[16,2048]{1,0:T(8,128)}, u32[]{:S(2)}) copy-start(f32[16,2048]{1,0:T(8,128)} %copy-done) | copy-start | bytes 393220 | tf_op jit(solution)/shard_map/while
  433.5 10.5 %copy-start.3 = (f32[4,64,2048]{2,1,0:T(8,128)S(1)}, f32[4,64,2048]{2,1,0:T(8,128)}, u32[]{:S(2)}) copy-start(f32[4,64,2048]{2,1,0:T(8,128)} %copy-done.2) | copy-start | bytes 6291460 | tf_op jit(solution)/shard_map/while
  433.5 10.5 %copy-start.6 = (f32[16,2048]{1,0:T(8,128)S(1)}, f32[16,2048]{1,0:T(8,128)}, u32[]{:S(2)}) copy-start(f32[16,2048]{1,0:T(8,128)} %copy-done.5) | copy-start | bytes 393220 | tf_op jit(solution)/shard_map/while
  433.5 10.4 %copy-start.8 = (f32[16,2048]{1,0:T(8,128)S(1)}, f32[16,2048]{1,0:T(8,128)}, u32[]{:S(2)}) copy-start(f32[16,2048]{1,0:T(8,128)} %copy-done.7) | copy-start | bytes 393220 | tf_op jit(solution)/shard_map/while
  444.4 4.2 copy-start
  510.1 8.4 %copy-start.9 = (f32[2,16,8,128]{3,1,2,0:T(8,128)S(1)}, f32[2,16,8,128]{3,1,2,0:T(8,128)}, u32[]{:S(2)}) copy-start(f32[2,16,8,128]{3,1,2,0:T(8,128)} %copy.35) | copy-start | bytes 393220 | tf_op jit(solution)/shard_map/while
  518.5 9.5 %copy-start.13 = (f32[16,2048]{1,0:T(8,128)S(1)}, f32[16,2048]{1,0:T(8,128)}, u32[]{:S(2)}) copy-start(f32[16,2048]{1,0:T(8,128)} %get-tuple-element.1006) | copy-start | bytes 393220 | tf_op jit(solution)/shard_map/while
  518.5 10.4 %copy-start.1 = (f32[16,2048]{1,0:T(8,128)S(1)}, f32[16,2048]{1,0:T(8,128)}, u32[]{:S(2)}) copy-start(f32[16,2048]{1,0:T(8,128)} %copy-done) | copy-start | bytes 393220 | tf_op jit(solution)/shard_map/while
  518.5 10.4 %copy-start.3 = (f32[4,64,2048]{2,1,0:T(8,128)S(1)}, f32[4,64,2048]{2,1,0:T(8,128)}, u32[]{:S(2)}) copy-start(f32[4,64,2048]{2,1,0:T(8,128)} %copy-done.2) | copy-start | bytes 6291460 | tf_op jit(solution)/shard_map/while
  518.5 10.4 %copy-start.6 = (f32[16,2048]{1,0:T(8,128)S(1)}, f32[16,2048]{1,0:T(8,128)}, u32[]{:S(2)}) copy-start(f32[16,2048]{1,0:T(8,128)} %copy-done.5) | copy-start | bytes 393220 | tf_op jit(solution)/shard_map/while
  518.6 10.4 %copy-start.8 = (f32[16,2048]{1,0:T(8,128)S(1)}, f32[16,2048]{1,0:T(8,128)}, u32[]{:S(2)}) copy-start(f32[16,2048]{1,0:T(8,128)} %copy-done.7) | copy-start | bytes 393220 | tf_op jit(solution)/shard_map/while
  595.2 8.2 %copy-start.9 = (f32[2,16,8,128]{3,1,2,0:T(8,128)S(1)}, f32[2,16,8,128]{3,1,2,0:T(8,128)}, u32[]{:S(2)}) copy-start(f32[2,16,8,128]{3,1,2,0:T(8,128)} %copy.35) | copy-start | bytes 393220 | tf_op jit(solution)/shard_map/while
  603.3 9.5 %copy-start.13 = (f32[16,2048]{1,0:T(8,128)S(1)}, f32[16,2048]{1,0:T(8,128)}, u32[]{:S(2)}) copy-start(f32[16,2048]{1,0:T(8,128)} %get-tuple-element.1006) | copy-start | bytes 393220 | tf_op jit(solution)/shard_map/while
  603.3 10.5 %copy-start.1 = (f32[16,2048]{1,0:T(8,128)S(1)}, f32[16,2048]{1,0:T(8,128)}, u32[]{:S(2)}) copy-start(f32[16,2048]{1,0:T(8,128)} %copy-done) | copy-start | bytes 393220 | tf_op jit(solution)/shard_map/while
  603.3 10.5 %copy-start.3 = (f32[4,64,2048]{2,1,0:T(8,128)S(1)}, f32[4,64,2048]{2,1,0:T(8,128)}, u32[]{:S(2)}) copy-start(f32[4,64,2048]{2,1,0:T(8,128)} %copy-done.2) | copy-start | bytes 6291460 | tf_op jit(solution)/shard_map/while
  603.3 10.5 %copy-start.6 = (f32[16,2048]{1,0:T(8,128)S(1)}, f32[16,2048]{1,0:T(8,128)}, u32[]{:S(2)}) copy-start(f32[16,2048]{1,0:T(8,128)} %copy-done.5) | copy-start | bytes 393220 | tf_op jit(solution)/shard_map/while
  603.3 10.5 %copy-start.8 = (f32[16,2048]{1,0:T(8,128)S(1)}, f32[16,2048]{1,0:T(8,128)}, u32[]{:S(2)}) copy-start(f32[16,2048]{1,0:T(8,128)} %copy-done.7) | copy-start | bytes 393220 | tf_op jit(solution)/shard_map/while
  656.4 1.4 collective-permute-start
  657.8 22.1 %collective-permute-start.1 = (f32[16,2048]{1,0:T(8,128)S(1)}, f32[16,2048]{1,0:T(8,128)S(1)}, u32[]{:S(2)}, u32[]{:S(2)}) collective-permute-start(f32[16,2048]{1,0:T(8,128)S(1)} %add.153), channel_id=1, source_target_pairs={{0,8},{4,12},{8,0},{12,4},{16,24},{20,28},{24,16},{28,20},{1,9},{5... | collective-permute-start | bytes 393224 | tf_op jit(solution)/shard_map/ppermute | solution.py:111
  659.3 21.2 %copy-start.11 = (f32[4,64,2048]{2,1,0:T(8,128)S(1)}, f32[4,64,2048]{2,1,0:T(8,128)}, u32[]{:S(2)}) copy-start(f32[4,64,2048]{2,1,0:T(8,128)} %get-tuple-element.500) | copy-start | bytes 6291460
  659.3 21.2 %copy-start.12 = (f32[4,64,2048]{2,1,0:T(8,128)S(1)}, f32[4,64,2048]{2,1,0:T(8,128)}, u32[]{:S(2)}) copy-start(f32[4,64,2048]{2,1,0:T(8,128)} %get-tuple-element.497) | copy-start | bytes 6291460
  659.3 21.2 %copy-start.15 = (bf16[256,2048]{1,0:T(8,128)(2,1)S(1)}, bf16[256,2048]{1,0:T(8,128)(2,1)}, u32[]{:S(2)}) copy-start(bf16[256,2048]{1,0:T(8,128)(2,1)} %param.17) | copy-start | bytes 3145732
  659.4 21.2 %copy-start.16 = (bf16[256,2048]{1,0:T(8,128)(2,1)S(1)}, bf16[256,2048]{1,0:T(8,128)(2,1)}, u32[]{:S(2)}) copy-start(bf16[256,2048]{1,0:T(8,128)(2,1)} %param.18) | copy-start | bytes 3145732
  659.4 21.2 %copy-start.17 = (f32[256,2048]{1,0:T(8,128)S(1)}, f32[256,2048]{1,0:T(8,128)}, u32[]{:S(2)}) copy-start(f32[256,2048]{1,0:T(8,128)} %get-tuple-element.788) | copy-start | bytes 6291460
  659.4 21.2 %copy-start.19 = (f32[256]{0:T(256)S(1)}, f32[256]{0:T(256)}, u32[]{:S(2)}) copy-start(f32[256]{0:T(256)} %copy-done.18) | copy-start | bytes 3076
  679.9 5.4 collective-permute-start.2
  (13 other events, 35.7 us)
Sparse Core Ops, SparseCore 0:
  9.6 83.4 all-gather.8
  94.9 159.1 all-gather.10
  256.6 23.3 all-gather.12
  282.3 23.3 all-gather.14
  618.3 23.3 all-gather.16
